TPU v7x, 32 devices: a whole 2x2x4 slice. The times are simulated.
32 devices in a mesh: dom: 8 (over z, y), rhs: 4 (over x, core).
Axes of the slice: x: 2, y: 2, z: 4, core: 2. Of those that a mesh axis runs over, the one named last changes fastest.
Arguments:
- tile_values: float32 [2048, 128, 128], P(('dom', 'rhs')), may hold values from -1 to 3, as said below
- tile_rows: int32 [2048], P(('dom', 'rhs')), may hold values from -1 to 31, as said below
- tile_cols: int32 [2048], P(('dom', 'rhs')), may hold values from 0 to 39, as said below
- send_lists: int32 [8, 2, 4], P('dom'), may hold values from 0 to 31, as said below
- replace_flags: int32 [4], replicated, may hold values from 0 to 1, as said below
- right_side: float32 [4, 256, 128], P(None, ('dom', 'rhs')), may hold values from -25 to 25
- start_iterate: float32 [4, 256, 128], P(None, ('dom', 'rhs')), may hold values from -25 to 25
- start_residual: float32 [4, 256, 128], P(None, ('dom', 'rhs')), may hold values from -25 to 25
- start_direction: float32 [4, 256, 128], P(None, ('dom', 'rhs')), may hold values from -25 to 25
Outputs:
- new_iterate: float32 [4, 256, 128], P(None, ('dom', 'rhs'))
- new_residual: float32 [4, 256, 128], P(None, ('dom', 'rhs'))
- new_direction: float32 [4, 256, 128], P(None, ('dom', 'rhs'))
Inputs may be any that keep to these rules, and one draw needn't show every extreme that they name: `tile_values`: the matrix assembled from all used tile slots is symmetric positive definite. `tile_rows`: -1 marks an empty slot; a used slot of the device with indices (d, r) names a block row from r * 8 to (r + 1) * 8 - 1 of partition d. `tile_cols`: 0 in empty slots. `send_lists`: the 8 entries of one partition are distinct. `replace_flags`: at least one load case is flagged and at least one is not.
All inputs are finite; a program needn't handle non-finite values.
Results may differ from a plain program's by a relative error of at most 0.0003.
Values sent between devices are 32-bit elements; how exact they have to be, the bound alone decides.
A program may use at most 64 MiB of HBM per device.

v0:
```python
import jax
import jax.numpy as jnp
import numpy as np
from jax import lax
from jax.sharding import PartitionSpec as P

SSTEP = 3


highest = lax.Precision.HIGHEST


def with_halo(x, sides, width):
    for axis, dim in sides:
        size, length = (lax.axis_size(axis), x.shape[dim])
        up = [(i, (i + 1) % size) for i in range(size - 1)]
        down = [(j, i) for i, j in up]
        last = lax.slice_in_dim(x, length - width, length, axis=dim)
        first = lax.slice_in_dim(x, 0, width, axis=dim)
        before = lax.ppermute(last, axis, up)
        after = lax.ppermute(first, axis, down)
        x = jnp.concatenate([before, x, after], axis=dim)
    return x


def shift_table(basis_steps):
    basis_width = 2 * basis_steps + 1
    shift_matrix = np.zeros((basis_width, basis_width), np.float32)
    for position in range(basis_steps):
        shift_matrix[position + 1, position] = 1.0
    for position in range(basis_steps - 1):
        shift_matrix[basis_steps + 2 + position, basis_steps + 1 + position] = 1.0
    return shift_matrix


def coefficients(gram_matrix, basis_steps):
    shift_matrix = jnp.asarray(shift_table(basis_steps))
    case_count = gram_matrix.shape[0]
    basis_width = gram_matrix.shape[1]
    eye_matrix = jnp.eye(basis_width, dtype=jnp.float32)
    direction = jnp.broadcast_to(eye_matrix[0], (case_count, basis_width))
    residual = jnp.broadcast_to(eye_matrix[basis_steps + 1], (case_count, basis_width))
    iterate = jnp.zeros((case_count, basis_width), jnp.float32)

    def quadratic(first_vec, second_vec):
        return jnp.einsum("ci,cij,cj->c", first_vec, gram_matrix, second_vec, precision=highest)

    res_norm = quadratic(residual, residual)
    for inner_step in range(basis_steps):
        mapped = jnp.einsum("ij,cj->ci", shift_matrix, direction, precision=highest)
        step_size = res_norm / quadratic(direction, mapped)
        iterate = iterate + step_size[:, None] * direction
        residual = residual - step_size[:, None] * mapped
        next_norm = quadratic(residual, residual)
        direction = residual + (next_norm / res_norm)[:, None] * direction
        res_norm = next_norm
    return (iterate, residual, direction)


def combine(basis_stack, weights):
    return jnp.einsum("icbt,ci->cbt", basis_stack, weights, precision=highest)


def multiply(extended, tile_values, tile_rows, tile_cols, row_start, row_count):
    picked = jnp.take(extended, tile_cols, axis=2)
    product = jnp.einsum("tij,kctj->kcti", tile_values, picked, precision=highest)
    wanted = row_start + lax.iota(jnp.int32, row_count)
    onehot = (tile_rows[:, None] == wanted[None, :]).astype(jnp.float32)
    return jnp.einsum("tb,kcti->kcbi", onehot, product, precision=highest)


def extend(whole_part, own_sends, ghost_width):
    outgoing = jnp.take(whole_part, own_sends, axis=2)
    ghost_rims = with_halo(outgoing, (("dom", 2),), ghost_width)
    return jnp.concatenate(
        [whole_part, ghost_rims[:, :, :ghost_width], ghost_rims[:, :, -ghost_width:]], axis=2
    )


def basis_from(apply_operator, direction, residual, carried):
    direction_powers = [direction]
    residual_powers = [residual]
    carried_image = None
    for power_step in range(SSTEP):
        members = [direction_powers[-1]]
        if power_step < SSTEP - 1:
            members.append(residual_powers[-1])
        if power_step == 0:
            members = members + carried
        mapped = apply_operator(jnp.stack(members))
        direction_powers.append(mapped[0])
        if power_step < SSTEP - 1:
            residual_powers.append(mapped[1])
        if power_step == 0 and carried:
            carried_image = mapped[-1]
    return (jnp.stack(direction_powers + residual_powers), carried_image)


def body(
    tile_values,
    tile_rows,
    tile_cols,
    send_lists,
    replace_flags,
    right_side,
    start_iterate,
    start_residual,
    start_direction,
):
    ghost_width = send_lists.shape[2]
    own_sends = send_lists[0].reshape(2 * ghost_width)
    own_rows = start_residual.shape[1]
    right_part, iterate_part, residual_part, direction_part = (
        right_side,
        start_iterate,
        start_residual,
        start_direction,
    )
    row_start = lax.axis_index("rhs") * own_rows

    def apply_operator(stacked):
        whole_part = lax.all_gather(stacked, "rhs", axis=2, tiled=True)
        return multiply(
            extend(whole_part, own_sends, ghost_width),
            tile_values,
            tile_rows,
            tile_cols,
            row_start,
            own_rows,
        )

    basis_stack, start_image = basis_from(
        apply_operator, direction_part, residual_part, [iterate_part]
    )
    gram_matrix = lax.psum(
        jnp.einsum("icbt,jcbt->cij", basis_stack, basis_stack, precision=highest), ("dom", "rhs")
    )
    iterate_coef, residual_coef, direction_coef = coefficients(gram_matrix, SSTEP)
    new_iterate = iterate_part + combine(basis_stack, iterate_coef)
    recursive = combine(basis_stack, residual_coef)
    new_direction = combine(basis_stack, direction_coef)
    shifted = jnp.einsum(
        "ij,cj->ci", jnp.asarray(shift_table(SSTEP)), iterate_coef, precision=highest
    )
    iterate_image = start_image + combine(basis_stack, shifted)
    replaced = right_part - iterate_image
    new_residual = jnp.where(replace_flags[:, None, None] > 0, replaced, recursive)
    return (new_iterate, new_residual, new_direction)


def solution(mesh):
    placed = (
        P(("dom", "rhs"), None, None),
        P(("dom", "rhs")),
        P(("dom", "rhs")),
        P("dom", None, None),
        P(),
        P(None, ("dom", "rhs"), None),
        P(None, ("dom", "rhs"), None),
        P(None, ("dom", "rhs"), None),
        P(None, ("dom", "rhs"), None),
    )
    return jax.shard_map(
        body,
        mesh=mesh,
        in_specs=placed,
        out_specs=(
            P(None, ("dom", "rhs"), None),
            P(None, ("dom", "rhs"), None),
            P(None, ("dom", "rhs"), None),
        ),
        check_vma=False,
    )
```

profile of v0, /device:TPU:0, one launch (start us, length us, event | category | flops | bytes accessed | tf_op | source)
XLA Modules:
  0.0 127.8 jit_solution(9150678838584309851)
XLA Ops:
  0.6 0.8 reshape_squeeze.6
  1.4 0.8 reshape_squeeze.5
  2.2 0.8 pad_maximum_fusion.2
  2.9 6.8 %all_gather.9 = f32[3,4,32,128]{3,2,1,0:T(8,128)S(1)} all-gather(f32[3,4,8,128]{3,2,1,0:T(8,128)S(1)} %pad_maximum_fusion.2), channel_id=1, replica_groups=mesh['dom'=8,'rhs'=4] {'rhs'}, dimensions={2}, use_global_device_ids=true | all-gather | bytes 245760 | tf_op jit(solution)/shard_map/all_gather | solution.py:122
  10.6 3.6 %collective-permute-start = (f32[3,4,4,128]{3,2,1,0:T(4,128)S(1)}, f32[3,4,4,128]{3,2,1,0:T(4,128)S(1)}, u32[]{:S(2)}, u32[]{:S(2)}) collective-permute-start(f32[3,4,4,128]{3,2,1,0:T(4,128)S(1)} %get-tuple-element.3), channel_id=1, source_target_pairs={{0,4},{4,8},{8,12},{12,16},{16,20},{20,24},{24,28},{1,5},{5,9},{9,... | collective-permute-start | bytes 73736 | tf_op jit(solution)/shard_map/ppermute | solution.py:20
  14.3 1.3 %collective-permute-start.1 = (f32[3,4,4,128]{3,2,1,0:T(4,128)S(1)}, f32[3,4,4,128]{3,2,1,0:T(4,128)S(1)}, u32[]{:S(2)}, u32[]{:S(2)}) collective-permute-start(f32[3,4,4,128]{3,2,1,0:T(4,128)S(1)} %get-tuple-element.4), channel_id=1, source_target_pairs={{4,0},{8,4},{12,8},{16,12},{20,16},{24,20},{28,24},{5,1},{9,5},{13... | collective-permute-start | bytes 73736 | tf_op jit(solution)/shard_map/ppermute | solution.py:21
  16.9 0.7 constant_dynamic-update-slice_fusion.2
  17.6 2.3 %collective-permute-done.1 = f32[3,4,4,128]{3,2,1,0:T(4,128)S(1)} collective-permute-done((f32[3,4,4,128]{3,2,1,0:T(4,128)S(1)}, f32[3,4,4,128]{3,2,1,0:T(4,128)S(1)}, u32[]{:S(2)}, u32[]{:S(2)}) %collective-permute-start.1) | collective-permute-done | bytes 24608 | tf_op jit(solution)/shard_map/ppermute | solution.py:21
  20.1 0.8 gather_fusion.1
  20.9 8.7 %fusion.2 = f32[64,3,4,128]{3,2,1,0:T(4,128)S(1)} fusion(f32[64,128,128]{2,1,0:T(8,128)} %param.11, f32[64,3,4,128]{3,2,1,0:T(4,128)S(1)} %gather_fusion.1, pred[64]{0:T(512)(128)(4,1)S(1)} %compare_and_fusion.1), kind=kOutput, calls=%fused_computation.8 | convolution fusion | flops 151093248 | bytes 4980800 | tf_op jit(solution)/shard_map/tij,kctj->kcti/dot_general | solution.py:66
  29.9 5.4 %all_gather.10 = f32[2,4,32,128]{3,2,1,0:T(8,128)S(1)} all-gather(f32[2,4,8,128]{3,2,1,0:T(8,128)S(1)} %stack.26), channel_id=1, replica_groups=mesh['dom'=8,'rhs'=4] {'rhs'}, dimensions={2}, use_global_device_ids=true | all-gather | bytes 163840 | tf_op jit(solution)/shard_map/all_gather | solution.py:122
  36.1 4.3 %collective-permute-start.2 = (f32[2,4,4,128]{3,2,1,0:T(4,128)S(1)}, f32[2,4,4,128]{3,2,1,0:T(4,128)S(1)}, u32[]{:S(2)}, u32[]{:S(2)}) collective-permute-start(f32[2,4,4,128]{3,2,1,0:T(4,128)S(1)} %get-tuple-element.7), channel_id=1, source_target_pairs={{0,4},{4,8},{8,12},{12,16},{16,20},{20,24},{24,28},{1,5},{5,9},{9,... | collective-permute-start | bytes 49160 | tf_op jit(solution)/shard_map/ppermute | solution.py:20
  40.4 1.3 %collective-permute-start.3 = (f32[2,4,4,128]{3,2,1,0:T(4,128)S(1)}, f32[2,4,4,128]{3,2,1,0:T(4,128)S(1)}, u32[]{:S(2)}, u32[]{:S(2)}) collective-permute-start(f32[2,4,4,128]{3,2,1,0:T(4,128)S(1)} %get-tuple-element.8), channel_id=1, source_target_pairs={{4,0},{8,4},{12,8},{16,12},{20,16},{24,20},{28,24},{5,1},{9,5},{13... | collective-permute-start | bytes 49160 | tf_op jit(solution)/shard_map/ppermute | solution.py:21
  41.8 4.2 %collective-permute-done.3 = f32[2,4,4,128]{3,2,1,0:T(4,128)S(1)} collective-permute-done((f32[2,4,4,128]{3,2,1,0:T(4,128)S(1)}, f32[2,4,4,128]{3,2,1,0:T(4,128)S(1)}, u32[]{:S(2)}, u32[]{:S(2)}) %collective-permute-start.3) | collective-permute-done | bytes 16416 | tf_op jit(solution)/shard_map/ppermute | solution.py:21
  46.1 0.7 gather_fusion.3
  46.9 8.4 %fusion = f32[64,2,4,128]{3,2,1,0:T(4,128)S(1)} fusion(f32[64,128,128]{2,1,0:T(8,128)} %param.11, f32[64,2,4,128]{3,2,1,0:T(4,128)S(1)} %gather_fusion.3, pred[64]{0:T(512)(128)(4,1)S(1)} %compare_and_fusion.1), kind=kOutput, calls=%fused_computation.6 | convolution fusion | flops 100728832 | bytes 4718656 | tf_op jit(solution)/shard_map/tij,kctj->kcti/dot_general | solution.py:66
  55.5 5.2 %all_gather.11 = f32[1,4,32,128]{3,2,1,0:T(8,128)S(1)} all-gather(f32[1,4,8,128]{3,2,1,0:T(8,128)S(1)} %get-tuple-element.5), channel_id=1, replica_groups=mesh['dom'=8,'rhs'=4] {'rhs'}, dimensions={2}, use_global_device_ids=true | all-gather | bytes 81920 | tf_op jit(solution)/shard_map/all_gather | solution.py:122
  61.5 3.4 %collective-permute-start.4 = (f32[1,4,4,128]{3,2,1,0:T(4,128)S(1)}, f32[1,4,4,128]{3,2,1,0:T(4,128)S(1)}, u32[]{:S(2)}, u32[]{:S(2)}) collective-permute-start(f32[1,4,4,128]{3,2,1,0:T(4,128)S(1)} %get-tuple-element.9), channel_id=1, source_target_pairs={{0,4},{4,8},{8,12},{12,16},{16,20},{20,24},{24,28},{1,5},{5,9},{9,... | collective-permute-start | bytes 24584 | tf_op jit(solution)/shard_map/ppermute | solution.py:20
  64.9 1.3 %collective-permute-start.5 = (f32[1,4,4,128]{3,2,1,0:T(4,128)S(1)}, f32[1,4,4,128]{3,2,1,0:T(4,128)S(1)}, u32[]{:S(2)}, u32[]{:S(2)}) collective-permute-start(f32[1,4,4,128]{3,2,1,0:T(4,128)S(1)} %get-tuple-element.10), channel_id=1, source_target_pairs={{4,0},{8,4},{12,8},{16,12},{20,16},{24,20},{28,24},{5,1},{9,5},{13... | collective-permute-start | bytes 24584 | tf_op jit(solution)/shard_map/ppermute | solution.py:21
  66.3 4.2 %collective-permute-done.5 = f32[1,4,4,128]{3,2,1,0:T(4,128)S(1)} collective-permute-done((f32[1,4,4,128]{3,2,1,0:T(4,128)S(1)}, f32[1,4,4,128]{3,2,1,0:T(4,128)S(1)}, u32[]{:S(2)}, u32[]{:S(2)}) %collective-permute-start.5) | collective-permute-done | bytes 8224 | tf_op jit(solution)/shard_map/ppermute | solution.py:21
  71.2 8.4 %convolution_bitcast_fusion = f32[4,64,128]{2,0,1:T(4,128)S(1)} fusion(f32[64,128,128]{2,1,0:T(8,128)} %param.11, f32[64,4,128]{2,1,0:T(4,128)S(1)} %gather_fusion.5, pred[64]{0:T(512)(128)(4,1)S(1)} %compare_and_fusion.1), kind=kOutput, calls=%fused_computation.10 | convolution fusion | flops 50364416 | bytes 4456512 | tf_op jit(solution)/shard_map/tij,kctj->kcti/dot_general | solution.py:66
  80.2 41.2 %psum.7 = f32[4,7,7]{2,1,0:T(8,128)S(1)} all-reduce(f32[4,7,7]{2,1,0:T(8,128)S(1)} %convolution_bitcast_fusion.3), channel_id=1, replica_groups=mesh['dom'=8,'rhs'=4] {'dom','rhs'}, use_global_device_ids=true, to_apply=%region_0.1 | all-reduce | flops 196 | bytes 1568 | tf_op jit(solution)/shard_map/psum | solution.py:135
  124.4 0.9 fusion.15
  127.1 0.7 fusion.35
  (87 shorter events, 10.4 us)
Async XLA Ops:
  0.6 29.0 %copy-start.4 = (s32[64]{0:T(128)S(1)}, s32[64]{0:T(128)}, u32[]{:S(2)}) copy-start(s32[64]{0:T(128)} %param.12) | copy-start | bytes 772
  10.6 7.0 %collective-permute-start = (f32[3,4,4,128]{3,2,1,0:T(4,128)S(1)}, f32[3,4,4,128]{3,2,1,0:T(4,128)S(1)}, u32[]{:S(2)}, u32[]{:S(2)}) collective-permute-start(f32[3,4,4,128]{3,2,1,0:T(4,128)S(1)} %get-tuple-element.3), channel_id=1, source_target_pairs={{0,4},{4,8},{8,12},{12,16},{16,20},{20,24},{24,28},{1,5},{5,9},{9,... | collective-permute-start | bytes 73736 | tf_op jit(solution)/shard_map/ppermute | solution.py:20
  14.3 5.7 %collective-permute-start.1 = (f32[3,4,4,128]{3,2,1,0:T(4,128)S(1)}, f32[3,4,4,128]{3,2,1,0:T(4,128)S(1)}, u32[]{:S(2)}, u32[]{:S(2)}) collective-permute-start(f32[3,4,4,128]{3,2,1,0:T(4,128)S(1)} %get-tuple-element.4), channel_id=1, source_target_pairs={{4,0},{8,4},{12,8},{16,12},{20,16},{24,20},{28,24},{5,1},{9,5},{13... | collective-permute-start | bytes 73736 | tf_op jit(solution)/shard_map/ppermute | solution.py:21
  29.6 36.6 %copy-start.5 = (s32[4]{0:T(128)S(1)}, s32[4]{0:T(128)}, u32[]{:S(2)}) copy-start(s32[4]{0:T(128)} %param.15) | copy-start | bytes 52
  36.1 5.8 %collective-permute-start.2 = (f32[2,4,4,128]{3,2,1,0:T(4,128)S(1)}, f32[2,4,4,128]{3,2,1,0:T(4,128)S(1)}, u32[]{:S(2)}, u32[]{:S(2)}) collective-permute-start(f32[2,4,4,128]{3,2,1,0:T(4,128)S(1)} %get-tuple-element.7), channel_id=1, source_target_pairs={{0,4},{4,8},{8,12},{12,16},{16,20},{20,24},{24,28},{1,5},{5,9},{9,... | collective-permute-start | bytes 49160 | tf_op jit(solution)/shard_map/ppermute | solution.py:20
  40.4 5.6 %collective-permute-start.3 = (f32[2,4,4,128]{3,2,1,0:T(4,128)S(1)}, f32[2,4,4,128]{3,2,1,0:T(4,128)S(1)}, u32[]{:S(2)}, u32[]{:S(2)}) collective-permute-start(f32[2,4,4,128]{3,2,1,0:T(4,128)S(1)} %get-tuple-element.8), channel_id=1, source_target_pairs={{4,0},{8,4},{12,8},{16,12},{20,16},{24,20},{28,24},{5,1},{9,5},{13... | collective-permute-start | bytes 49160 | tf_op jit(solution)/shard_map/ppermute | solution.py:21
  46.8 32.9 %copy-start.2 = (f32[4,8,128]{2,1,0:T(8,128)S(1)}, f32[4,8,128]{2,1,0:T(8,128)}, u32[]{:S(2)}) copy-start(f32[4,8,128]{2,1,0:T(8,128)} %param.18) | copy-start | bytes 49156
  55.3 66.6 %copy-start.1 = (f32[7,7]{1,0:T(8,128)S(1)}, f32[7,7]{1,0:T(8,128)}, u32[]{:S(2)}) copy-start(f32[7,7]{1,0:T(8,128)} %constant.87.clone) | copy-start | bytes 592
  55.3 71.2 %copy-start = (f32[4,8,128]{2,1,0:T(8,128)S(1)}, f32[4,8,128]{2,1,0:T(8,128)}, u32[]{:S(2)}) copy-start(f32[4,8,128]{2,1,0:T(8,128)} %param.17) | copy-start | bytes 49156
  55.3 71.8 %copy-start.3 = (f32[4,8,128]{2,1,0:T(8,128)S(1)}, f32[4,8,128]{2,1,0:T(8,128)}, u32[]{:S(2)}) copy-start(f32[4,8,128]{2,1,0:T(8,128)} %param.16) | copy-start | bytes 49156
  61.5 4.8 %collective-permute-start.4 = (f32[1,4,4,128]{3,2,1,0:T(4,128)S(1)}, f32[1,4,4,128]{3,2,1,0:T(4,128)S(1)}, u32[]{:S(2)}, u32[]{:S(2)}) collective-permute-start(f32[1,4,4,128]{3,2,1,0:T(4,128)S(1)} %get-tuple-element.9), channel_id=1, source_target_pairs={{0,4},{4,8},{8,12},{12,16},{16,20},{20,24},{24,28},{1,5},{5,9},{9,... | collective-permute-start | bytes 24584 | tf_op jit(solution)/shard_map/ppermute | solution.py:20
  64.9 5.5 %collective-permute-start.5 = (f32[1,4,4,128]{3,2,1,0:T(4,128)S(1)}, f32[1,4,4,128]{3,2,1,0:T(4,128)S(1)}, u32[]{:S(2)}, u32[]{:S(2)}) collective-permute-start(f32[1,4,4,128]{3,2,1,0:T(4,128)S(1)} %get-tuple-element.10), channel_id=1, source_target_pairs={{4,0},{8,4},{12,8},{16,12},{20,16},{24,20},{28,24},{5,1},{9,5},{13... | collective-permute-start | bytes 24584 | tf_op jit(solution)/shard_map/ppermute | solution.py:21
where the time goes:
time: 128 us
  blocking collectives  58.7 us (46%)
  matrix products  30.5 us (24%)
  starting transfers between devices  15.3 us (12%)
  waiting for transfers between devices  10.9 us (9%)
  local copies, waits for them, and re-layouts  6.71 us (5%)
  other arithmetic  4.71 us (4%)
    psum x1, blocking collectives, body(): lax.psum(jnp.einsum('icbt,jcbt->cij', basis_stack, basis_stack, precision...  41.2 us
    dot_general x3, matrix products, multiply(): jnp.einsum('tij,kctj->kcti', tile_values, picked, precision=highest)  25.5 us
    all_gather x3, blocking collectives, apply_operator(): whole_part = lax.all_gather(stacked, 'rhs', axis=2, tiled=True)  17.5 us
    ppermute x3, starting transfers between devices, with_halo(): before = lax.ppermute(last, axis, up)  11.4 us
    ppermute x3, waiting for transfers between devices, with_halo(): after = lax.ppermute(first, axis, down)  10.7 us
    ppermute x3, starting transfers between devices, with_halo(): after = lax.ppermute(first, axis, down)  3.88 us
  transfers between devices with their start and end apart: 6, of which 4 were waited for; matrix products, arithmetic and copies ran while one was open for 2% of the time, Pallas kernels for 0%

commit v1 on v0

v1 whole, which is shorter than its diff:
```python
import functools

import jax
import jax.numpy as jnp
from jax import lax
from jax.experimental import pallas as pl
from jax.experimental.pallas import tpu as pltpu
from jax.sharding import PartitionSpec as P

SSTEP = 3
WIDTH = 2 * SSTEP + 1
P0, R0, X0, P1, R1, P2 = range(6)
SENT = 6
MESH = pl.DeviceIdType.MESH
UNROLL = 4
PAIRS = [(i, j) for i in range(WIDTH) for j in range(i, WIDTH)]
PAIR_LANE = {pair: lane for lane, pair in enumerate(PAIRS)}


def shifted_of(vec):
    return {i + 1: v for i, v in vec.items() if i not in (SSTEP, WIDTH - 1)}


def axpy(base, scale, other, sign):
    out = dict(base)
    for i, v in other.items():
        term = scale * v
        if i in out:
            out[i] = out[i] + term if sign > 0 else out[i] - term
        else:
            out[i] = term if sign > 0 else -term
    return out


def coefficients(gram):
    def quadratic(first, second):
        total = None
        for i, a in first.items():
            inner = None
            for j, b in second.items():
                term = gram[(min(i, j), max(i, j))] * b
                inner = term if inner is None else inner + term
            inner = inner * a
            total = inner if total is None else total + inner
        return total

    one = jnp.ones_like(gram[(0, 0)])
    direction = {0: one}
    residual = {SSTEP + 1: one}
    iterate = {}
    norm = quadratic(residual, residual)
    for _ in range(SSTEP):
        mapped = shifted_of(direction)
        step = norm / quadratic(direction, mapped)
        iterate = axpy(iterate, step, direction, 1)
        residual = axpy(residual, step, mapped, -1)
        next_norm = quadratic(residual, residual)
        direction = axpy(residual, next_norm / norm, direction, 1)
        norm = next_norm
    return iterate, residual, direction


def kernel(
    parts,
    split,
    rows_s,
    cols_s,
    sends_s,
    flags_s,
    tiles_h,
    right_h,
    iterate_h,
    residual_h,
    direction_h,
    iterate_o,
    residual_o,
    direction_o,
    *scratch,
):
    scratch = list(scratch)
    take = lambda n: [scratch.pop(0) for _ in range(n)]
    ext = take(SENT)
    own = take(SENT + 3)
    ghost_send = take(SENT)
    ghost_recv = take(SENT)
    tiles, weights, vec_in, gram_r, gram_d = take(5)
    tile_sem, vec_sem, peer_send, peer_recv, side_send, side_recv = take(6)
    gr_send, gr_recv, gd_send, gd_recv = take(4)

    d, r = lax.axis_index("dom"), lax.axis_index("rhs")
    cases, own_rows, tb = own[0].shape[1], own[0].shape[0], own[0].shape[2]
    gh = ghost_send[0].shape[1]
    tile_count = tiles.shape[0]
    chunks = tile_sem.shape[0]
    per_chunk = tile_count // chunks
    base = r * own_rows
    has_left, has_right = d > 0, d < parts - 1

    vec_copies = []
    for i, ref in enumerate((direction_h, residual_h, iterate_h, right_h)):
        copy = pltpu.make_async_copy(ref, vec_in.at[i], vec_sem.at[i])
        copy.start()
        vec_copies.append(copy)
    tile_copies = []
    for i in range(chunks):
        part = pl.ds(i * per_chunk, per_chunk)
        copy = pltpu.make_async_copy(tiles_h.at[part], tiles.at[part], tile_sem.at[i])
        copy.start()
        tile_copies.append(copy)

    barrier = pltpu.get_barrier_semaphore()

    def greet(dd, rr):
        pl.semaphore_signal(barrier, inc=1, device_id=(dd, rr), device_id_type=MESH)

    for o in range(1, split):
        greet(d, lax.rem(r + o, split))

    @pl.when(has_left)
    def _():
        for o in range(1, split):
            greet(d - 1, lax.rem(r + o, split))

    @pl.when(has_right)
    def _():
        for o in range(1, split):
            greet(d + 1, lax.rem(r + o, split))

    @pl.loop(1, parts)
    def _(o):
        greet(lax.rem(d + o, parts), r)

    sides = has_left.astype(jnp.int32) + has_right.astype(jnp.int32)

    def peer_copy(v, o):
        return pltpu.make_async_remote_copy(
            src_ref=own[v],
            dst_ref=ext[v].at[pl.ds(base, own_rows)],
            send_sem=peer_send.at[v, o - 1],
            recv_sem=peer_recv.at[v, o - 1],
            device_id=(d, lax.rem(r + o, split)),
            device_id_type=MESH,
        )

    def side_copy(v, side, o):
        return pltpu.make_async_remote_copy(
            src_ref=ghost_send[v].at[side],
            dst_ref=ghost_recv[v].at[1 - side, o],
            send_sem=side_send.at[v, side, o],
            recv_sem=side_recv.at[v, 1 - side, o],
            device_id=(d - 1 if side == 0 else d + 1, lax.rem(r + o, split)),
            device_id_type=MESH,
        )

    def stage(v, values):
        for b in range(own_rows):
            own[v][b] = values[b]
            ext[v][base + b] = values[b]
        for side in range(2):
            for k in range(gh):
                local = sends_s[0, side, k] - base
                value = own[v][jnp.clip(local, 0, own_rows - 1)]
                where = jnp.full((cases, tb), local, jnp.int32)
                ghost_send[v][side, k] = jnp.where(
                    (where >= 0) & (where < own_rows), value, 0.0
                )

    def send(v):
        @pl.when(has_left)
        def _():
            for o in range(split):
                side_copy(v, 0, o).start()

        @pl.when(has_right)
        def _():
            for o in range(split):
                side_copy(v, 1, o).start()

        for o in range(1, split):
            peer_copy(v, o).start()

    def receive(v):
        for o in range(1, split):
            peer_copy(v, o).wait_recv()
        for side, present in ((0, has_left), (1, has_right)):
            first = split * own_rows + side * gh

            @pl.when(present)
            def _():
                for o in range(split):
                    side_copy(v, 1 - side, o).wait_recv()
                for k in range(gh):
                    total = ghost_recv[v][side, 0, k]
                    for o in range(1, split):
                        total = total + ghost_recv[v][side, o, k]
                    ext[v][first + k] = total

            @pl.when(jnp.logical_not(present))
            def _():
                for k in range(gh):
                    ext[v][first + k] = jnp.zeros((cases, tb), jnp.float32)

    def sent(v):
        for o in range(1, split):
            peer_copy(v, o).wait_send()
        for side, present in ((0, has_left), (1, has_right)):

            @pl.when(present)
            def _():
                for o in range(split):
                    side_copy(v, side, o).wait_send()

    def input_blocks(i):
        return [vec_in[i, :, b, :] for b in range(own_rows)]

    low = lax.broadcasted_iota(jnp.int32, (2 * cases, tb), 0) < cases

    def apply_to(v):
        def step(i, acc):
            acc = list(acc)
            for u in range(UNROLL):
                q = i * UNROLL + u
                pair = jnp.concatenate(
                    [ext[v][cols_s[2 * q]], ext[v][cols_s[2 * q + 1]]], axis=0
                )
                high = pair.astype(jnp.bfloat16).astype(jnp.float32)
                lhs = jnp.concatenate([high, pair - high], axis=0).astype(jnp.bfloat16)
                lhs = jnp.concatenate([lhs, lhs], axis=1)
                out = jnp.dot(lhs, weights[q], preferred_element_type=jnp.float32)
                out = out[: 2 * cases] + out[2 * cases :]
                out = jnp.where(low, out[:, :tb], out[:, tb:])
                row = jnp.where(low, rows_s[2 * q], rows_s[2 * q + 1]) - base
                acc = [a + jnp.where(row == b, out, 0.0) for b, a in enumerate(acc)]
            return tuple(acc)

        zero = jnp.zeros((2 * cases, tb), jnp.float32)
        acc = lax.fori_loop(0, tile_count // 2 // UNROLL, step, (zero,) * own_rows)
        return [a[:cases] + a[cases:] for a in acc]

    for v in range(3):
        vec_copies[v].wait()
        stage(v, input_blocks(v))
    pl.semaphore_wait(barrier, split - 1 + parts - 1 + (split - 1) * sides)
    for v in range(3):
        send(v)

    for i in range(chunks):
        tile_copies[i].wait()

        @pl.loop(i * per_chunk // 2, (i + 1) * per_chunk // 2)
        def _(q):
            for h in range(2):
                flipped = tiles[2 * q + h].T
                high = flipped.astype(jnp.bfloat16)
                weights[q, :tb, h * tb : (h + 1) * tb] = high
                weights[q, tb:, h * tb : (h + 1) * tb] = (
                    flipped - high.astype(jnp.float32)
                ).astype(jnp.bfloat16)

    lanes = lax.broadcasted_iota(jnp.int32, (cases, tb), 1)
    basis = [own[P0], own[P1], own[P2], own[SENT], own[R0], own[R1], own[SENT + 1]]
    image = own[SENT + 2]

    def gram_of(payload, pairs):
        for i, j in pairs:
            total = basis[i][0] * basis[j][0]
            for b in range(1, own_rows):
                total = total + basis[i][b] * basis[j][b]
            total = jnp.sum(total, axis=1, keepdims=True)
            payload = payload + jnp.where(lanes == PAIR_LANE[(i, j)], total, 0.0)
        return payload

    def pairs_new(known, new):
        have = set(known) | set(new)
        return [p for p in PAIRS if set(p) <= have and set(p) & set(new)]

    receive(P0)
    stage(P1, apply_to(P0))
    send(P1)
    receive(R0)
    stage(R1, apply_to(R0))
    send(R1)
    receive(X0)
    for b, value in enumerate(apply_to(X0)):
        image[b] = value
    payload = jnp.zeros((cases, tb), jnp.float32)
    payload = gram_of(payload, pairs_new([], [0, 1, 4, 5]))
    receive(P1)
    stage(P2, apply_to(P1))
    send(P2)
    receive(R1)
    for b, value in enumerate(apply_to(R1)):
        own[SENT + 1][b] = value
    payload = gram_of(payload, pairs_new([0, 1, 4, 5], [2, 6]))
    receive(P2)
    for b, value in enumerate(apply_to(P2)):
        own[SENT][b] = value
    payload = gram_of(payload, pairs_new([0, 1, 2, 4, 5, 6], [3]))

    gram_r[r] = payload

    def gram_r_copy(o):
        return pltpu.make_async_remote_copy(
            src_ref=gram_r.at[r],
            dst_ref=gram_r.at[r],
            send_sem=gr_send.at[o - 1],
            recv_sem=gr_recv.at[o - 1],
            device_id=(d, lax.rem(r + o, split)),
            device_id_type=MESH,
        )

    for o in range(1, split):
        gram_r_copy(o).start()
    for o in range(1, split):
        gram_r_copy(o).wait()
    gram_d[d] = jnp.sum(gram_r[...], axis=0)

    def gram_d_copy(o):
        return pltpu.make_async_remote_copy(
            src_ref=gram_d.at[d],
            dst_ref=gram_d.at[d],
            send_sem=gd_send.at[o - 1],
            recv_sem=gd_recv.at[o - 1],
            device_id=(lax.rem(d + o, parts), r),
            device_id_type=MESH,
        )

    @pl.loop(1, parts)
    def _(o):
        gram_d_copy(o).start()

    for v in range(SENT):
        sent(v)
    vec_copies[3].wait()

    @pl.loop(1, parts)
    def _(o):
        gram_d_copy(o).wait()

    whole = jnp.sum(gram_d[...], axis=0)
    gram = {
        pair: jnp.broadcast_to(whole[:, lane : lane + 1], (cases, tb))
        for pair, lane in PAIR_LANE.items()
    }
    iterate_c, residual_c, direction_c = coefficients(gram)
    shifted_c = shifted_of(iterate_c)
    case_ids = lax.broadcasted_iota(jnp.int32, (cases, tb), 0)
    flags = jnp.zeros((cases, tb), jnp.int32)
    for c in range(cases):
        flags = jnp.where(case_ids == c, flags_s[c], flags)

    for b in range(own_rows):
        blocks = [ref[b] for ref in basis]

        def combine(weights_of):
            total = None
            for i, w in weights_of.items():
                total = blocks[i] * w if total is None else total + blocks[i] * w
            return total

        replaced = vec_in[3, :, b, :] - (image[b] + combine(shifted_c))
        iterate_o[:, b, :] = vec_in[2, :, b, :] + combine(iterate_c)
        residual_o[:, b, :] = jnp.where(flags > 0, replaced, combine(residual_c))
        direction_o[:, b, :] = combine(direction_c)


def body(parts, split, tiles, rows, cols, sends, flags, right, iterate, residual, direction):
    cases, own_rows, tb = residual.shape
    gh = sends.shape[2]
    count = tiles.shape[0]
    f32 = jnp.float32
    dma = pltpu.SemaphoreType.DMA
    smem = pl.BlockSpec(memory_space=pltpu.SMEM)
    hbm = pl.BlockSpec(memory_space=pl.ANY)
    vmem = pl.BlockSpec(memory_space=pltpu.VMEM)
    scratch = (
        [pltpu.VMEM((split * own_rows + 2 * gh, cases, tb), f32)] * SENT
        + [pltpu.VMEM((own_rows, cases, tb), f32)] * (SENT + 3)
        + [pltpu.VMEM((2, gh, cases, tb), f32)] * SENT
        + [pltpu.VMEM((2, split, gh, cases, tb), f32)] * SENT
        + [
            pltpu.VMEM((count, tb, tb), f32),
            pltpu.VMEM((count // 2, 2 * tb, 2 * tb), jnp.bfloat16),
            pltpu.VMEM((4, cases, own_rows, tb), f32),
            pltpu.VMEM((split, cases, tb), f32),
            pltpu.VMEM((parts, cases, tb), f32),
            dma((4,)),
            dma((4,)),
            dma((SENT, split - 1)),
            dma((SENT, split - 1)),
            dma((SENT, 2, split)),
            dma((SENT, 2, split)),
            dma((split - 1,)),
            dma((split - 1,)),
            dma((parts - 1,)),
            dma((parts - 1,)),
        ]
    )
    out = jax.ShapeDtypeStruct((cases, own_rows, tb), f32)
    return pl.pallas_call(
        functools.partial(kernel, parts, split),
        out_shape=(out, out, out),
        in_specs=[smem] * 4 + [hbm] * 5,
        out_specs=(vmem, vmem, vmem),
        scratch_shapes=scratch,
        compiler_params=pltpu.CompilerParams(
            collective_id=0, has_side_effects=True, vmem_limit_bytes=40 * 1024 * 1024
        ),
    )(rows, cols, sends, flags, tiles, right, iterate, residual, direction)


def solution(mesh):
    both = ("dom", "rhs")
    vec = P(None, both, None)
    placed = (P(both, None, None), P(both), P(both), P("dom", None, None), P(), vec, vec, vec, vec)
    return jax.shard_map(
        functools.partial(body, mesh.shape["dom"], mesh.shape["rhs"]),
        mesh=mesh,
        in_specs=placed,
        out_specs=(vec, vec, vec),
        check_vma=False,
    )
```

time: 128 us -> 42.4 us (0.33)
  blocking collectives: 58.7 us -> 0 us
  Pallas kernels: 0 us -> 31.7 us
  matrix products: 30.5 us -> 0 us
  starting transfers between devices: 15.3 us -> 0 us
  waiting for transfers between devices: 10.9 us -> 0 us
  other arithmetic: 4.71 us -> 0 us
  local copies, waits for them, and re-layouts: 6.71 us -> 9.51 us
    psum x1 -> x0, blocking collectives: 41.2 us -> none  [body(): lax.psum(jnp.einsum('icbt,jcbt->cij', basis_stack, basis_stack, precision...]
    pallas_call x0 -> x1, Pallas kernels: none -> 31.7 us  [body(): pl.pallas_call(functools.partial(kernel, parts, split), out_shape=(out, o...]
    dot_general x22 -> x0, matrix products: 30.5 us -> none  [the longest x3 25.5 us: multiply(): jnp.einsum('tij,kctj->kcti', tile_values, picked, precision=highest)]
    all_gather x3 -> x0, blocking collectives: 17.5 us -> none  [apply_operator(): whole_part = lax.all_gather(stacked, 'rhs', axis=2, tiled=True)]
    ppermute x6 -> x0, starting transfers between devices: 15.3 us -> none  [the longest x3 11.4 us: with_halo(): before = lax.ppermute(last, axis, up)]
    ppermute x6 -> x0, waiting for transfers between devices: 10.9 us -> none  [the longest x3 10.7 us: with_halo(): after = lax.ppermute(first, axis, down)]
    unnamed x16 -> x21, local copies, waits for them, and re-layouts: 0.76 us -> 9.51 us
    gather x6 -> x0, local copies, waits for them, and re-layouts: 3.99 us -> none  [the longest x3 2.24 us: multiply(): picked = jnp.take(extended, tile_cols, axis=2)]
  transfers between devices with their start and end apart: 6 -> 0, of which waited for: 4 -> 0; matrix products, arithmetic and copies ran while one was open for 2% -> 0% of each run, Pallas kernels for 0% -> 0%
where the time goes in v1:
time: 42.4 us; the launch traced here: 41.9 us
  Pallas kernels  31.7 us (75%)
  local copies, waits for them, and re-layouts  9.51 us (22%)
  between operations  0.66 us (2%)
    pallas_call x1, Pallas kernels, body(): pl.pallas_call(functools.partial(kernel, parts, split), out_shape=(out, o...  31.7 us
    unnamed x21, local copies, waits for them, and re-layouts  9.51 us

profile of v1, /device:TPU:0, one launch (start us, length us, event | category | flops | bytes accessed | tf_op | source)
XLA Modules:
  0.0 41.9 jit_solution(1263296230210146171)
XLA Ops:
  0.6 0.0 copy-start
  0.6 2.2 %copy-done = f32[64,128,128]{2,1,0:T(8,128)S(1)} copy-done((f32[64,128,128]{2,1,0:T(8,128)S(1)}, f32[64,128,128]{2,1,0:T(8,128)}, u32[]{:S(2)}) %copy-start) | copy-done | bytes 4194328
  2.8 0.0 copy-start.1
  2.8 0.7 %copy-done.1 = f32[4,8,128]{2,1,0:T(8,128)S(1)} copy-done((f32[4,8,128]{2,1,0:T(8,128)S(1)}, f32[4,8,128]{2,1,0:T(8,128)}, u32[]{:S(2)}) %copy-start.1) | copy-done | bytes 16408
  3.5 0.0 copy-start.2
  3.5 0.7 %copy-done.2 = f32[4,8,128]{2,1,0:T(8,128)S(1)} copy-done((f32[4,8,128]{2,1,0:T(8,128)S(1)}, f32[4,8,128]{2,1,0:T(8,128)}, u32[]{:S(2)}) %copy-start.2) | copy-done | bytes 16408
  4.3 0.0 copy-start.3
  4.3 0.7 %copy-done.3 = f32[4,8,128]{2,1,0:T(8,128)S(1)} copy-done((f32[4,8,128]{2,1,0:T(8,128)S(1)}, f32[4,8,128]{2,1,0:T(8,128)}, u32[]{:S(2)}) %copy-start.3) | copy-done | bytes 16408
  5.0 0.0 copy-start.4
  5.0 0.7 %copy-done.4 = f32[4,8,128]{2,1,0:T(8,128)S(1)} copy-done((f32[4,8,128]{2,1,0:T(8,128)S(1)}, f32[4,8,128]{2,1,0:T(8,128)}, u32[]{:S(2)}) %copy-start.4) | copy-done | bytes 16408
  5.7 0.0 copy-start.5
  5.7 0.7 %copy-done.5 = s32[1,2,4]{2,1,0:T(2,128)S(1)} copy-done((s32[1,2,4]{2,1,0:T(2,128)S(1)}, s32[1,2,4]{2,1,0:T(2,128)}, u32[]{:S(2)}) %copy-start.5) | copy-done | bytes 56
  6.4 0.0 copy-start.6
  6.4 0.7 %copy-done.6 = s32[64]{0:T(128)S(1)} copy-done((s32[64]{0:T(128)S(1)}, s32[64]{0:T(128)}, u32[]{:S(2)}) %copy-start.6) | copy-done | bytes 280
  7.0 0.0 copy-start.7
  7.0 0.7 %copy-done.7 = s32[64]{0:T(128)S(1)} copy-done((s32[64]{0:T(128)S(1)}, s32[64]{0:T(128)}, u32[]{:S(2)}) %copy-start.7) | copy-done | bytes 280
  7.7 0.0 copy-start.8
  7.7 0.7 %copy-done.8 = s32[4]{0:T(128)S(1)} copy-done((s32[4]{0:T(128)S(1)}, s32[4]{0:T(128)}, u32[]{:S(2)}) %copy-start.8) | copy-done | bytes 40
  8.3 31.7 %shard_map.112 = (f32[4,8,128]{2,1,0:T(8,128)S(1)}, f32[4,8,128]{2,1,0:T(8,128)S(1)}, f32[4,8,128]{2,1,0:T(8,128)S(1)}) custom-call(s32[64]{0:T(128)S(1)} %copy-done.6, s32[64]{0:T(128)S(1)} %copy-done.7, s32[1,2,4]{2,1,0:T(2,128)S(1)} %copy-done.5, s32[4]{0:T(128)S(1)} %copy-done.8, f32[64,128,128]{2,1,0:T(8,128)S(1)} %copy-done, ...), custom_call_target="tpu_custom_call" | custom-call | tf_op jit(solution)/shard_map/pallas_call | solution.py:400
  40.0 0.6 %copy.15 = f32[4,8,128]{2,1,0:T(8,128)} copy(f32[4,8,128]{2,1,0:T(8,128)S(1)} %get-tuple-element.6) | data formatting | bytes 32768
  40.6 0.6 %copy.16 = f32[4,8,128]{2,1,0:T(8,128)} copy(f32[4,8,128]{2,1,0:T(8,128)S(1)} %get-tuple-element.7) | data formatting | bytes 32768
  41.2 0.6 %copy.17 = f32[4,8,128]{2,1,0:T(8,128)} copy(f32[4,8,128]{2,1,0:T(8,128)S(1)} %get-tuple-element.8) | data formatting | bytes 32768
Async XLA Ops:
  0.6 2.2 %copy-start = (f32[64,128,128]{2,1,0:T(8,128)S(1)}, f32[64,128,128]{2,1,0:T(8,128)}, u32[]{:S(2)}) copy-start(f32[64,128,128]{2,1,0:T(8,128)} %tiles_h.1) | copy-start | bytes 12582916
  2.8 0.7 %copy-start.1 = (f32[4,8,128]{2,1,0:T(8,128)S(1)}, f32[4,8,128]{2,1,0:T(8,128)}, u32[]{:S(2)}) copy-start(f32[4,8,128]{2,1,0:T(8,128)} %right_h.1) | copy-start | bytes 49156
  3.5 0.7 %copy-start.2 = (f32[4,8,128]{2,1,0:T(8,128)S(1)}, f32[4,8,128]{2,1,0:T(8,128)}, u32[]{:S(2)}) copy-start(f32[4,8,128]{2,1,0:T(8,128)} %iterate_h.1) | copy-start | bytes 49156
  4.3 0.7 %copy-start.3 = (f32[4,8,128]{2,1,0:T(8,128)S(1)}, f32[4,8,128]{2,1,0:T(8,128)}, u32[]{:S(2)}) copy-start(f32[4,8,128]{2,1,0:T(8,128)} %residual_h.1) | copy-start | bytes 49156
  5.0 0.7 %copy-start.4 = (f32[4,8,128]{2,1,0:T(8,128)S(1)}, f32[4,8,128]{2,1,0:T(8,128)}, u32[]{:S(2)}) copy-start(f32[4,8,128]{2,1,0:T(8,128)} %direction_h.1) | copy-start | bytes 49156
  5.7 0.7 %copy-start.5 = (s32[1,2,4]{2,1,0:T(2,128)S(1)}, s32[1,2,4]{2,1,0:T(2,128)}, u32[]{:S(2)}) copy-start(s32[1,2,4]{2,1,0:T(2,128)} %sends_s.1) | copy-start | bytes 100
  6.4 0.7 %copy-start.6 = (s32[64]{0:T(128)S(1)}, s32[64]{0:T(128)}, u32[]{:S(2)}) copy-start(s32[64]{0:T(128)} %rows_s.1) | copy-start | bytes 772
  7.0 0.7 %copy-start.7 = (s32[64]{0:T(128)S(1)}, s32[64]{0:T(128)}, u32[]{:S(2)}) copy-start(s32[64]{0:T(128)} %cols_s.1) | copy-start | bytes 772
  7.7 0.7 %copy-start.8 = (s32[4]{0:T(128)S(1)}, s32[4]{0:T(128)}, u32[]{:S(2)}) copy-start(s32[4]{0:T(128)} %flags_s.1) | copy-start | bytes 52

commit v2 on v1

--- a/solution.py
+++ b/solution.py
@@ -12,7 +12,7 @@
 P0, R0, X0, P1, R1, P2 = range(6)
 SENT = 6
 MESH = pl.DeviceIdType.MESH
-UNROLL = 4
+UNROLL = 16
 PAIRS = [(i, j) for i in range(WIDTH) for j in range(i, WIDTH)]
 PAIR_LANE = {pair: lane for lane, pair in enumerate(PAIRS)}
 
@@ -66,15 +66,11 @@
     rows_s,
     cols_s,
     sends_s,
-    flags_s,
     tiles_h,
-    right_h,
     iterate_h,
     residual_h,
     direction_h,
-    iterate_o,
-    residual_o,
-    direction_o,
+    out_ref,
     *scratch,
 ):
     scratch = list(scratch)
@@ -97,7 +93,7 @@
     has_left, has_right = d > 0, d < parts - 1
 
     vec_copies = []
-    for i, ref in enumerate((direction_h, residual_h, iterate_h, right_h)):
+    for i, ref in enumerate((direction_h, residual_h, iterate_h)):
         copy = pltpu.make_async_copy(ref, vec_in.at[i], vec_sem.at[i])
         copy.start()
         vec_copies.append(copy)
@@ -331,7 +327,6 @@
 
     for v in range(SENT):
         sent(v)
-    vec_copies[3].wait()
 
     @pl.loop(1, parts)
     def _(o):
@@ -344,11 +339,6 @@
     }
     iterate_c, residual_c, direction_c = coefficients(gram)
     shifted_c = shifted_of(iterate_c)
-    case_ids = lax.broadcasted_iota(jnp.int32, (cases, tb), 0)
-    flags = jnp.zeros((cases, tb), jnp.int32)
-    for c in range(cases):
-        flags = jnp.where(case_ids == c, flags_s[c], flags)
-
     for b in range(own_rows):
         blocks = [ref[b] for ref in basis]
 
@@ -358,10 +348,10 @@
                 total = blocks[i] * w if total is None else total + blocks[i] * w
             return total
 
-        replaced = vec_in[3, :, b, :] - (image[b] + combine(shifted_c))
-        iterate_o[:, b, :] = vec_in[2, :, b, :] + combine(iterate_c)
-        residual_o[:, b, :] = jnp.where(flags > 0, replaced, combine(residual_c))
-        direction_o[:, b, :] = combine(direction_c)
+        out_ref[0, :, b, :] = combine(iterate_c)
+        out_ref[1, :, b, :] = image[b] + combine(shifted_c)
+        out_ref[2, :, b, :] = combine(residual_c)
+        out_ref[3, :, b, :] = combine(direction_c)
 
 
 def body(parts, split, tiles, rows, cols, sends, flags, right, iterate, residual, direction):
@@ -371,7 +361,7 @@
     f32 = jnp.float32
     dma = pltpu.SemaphoreType.DMA
     smem = pl.BlockSpec(memory_space=pltpu.SMEM)
-    hbm = pl.BlockSpec(memory_space=pl.ANY)
+    hbm = pl.BlockSpec(memory_space=pltpu.HBM)
     vmem = pl.BlockSpec(memory_space=pltpu.VMEM)
     scratch = (
         [pltpu.VMEM((split * own_rows + 2 * gh, cases, tb), f32)] * SENT
@@ -381,11 +371,11 @@
         + [
             pltpu.VMEM((count, tb, tb), f32),
             pltpu.VMEM((count // 2, 2 * tb, 2 * tb), jnp.bfloat16),
-            pltpu.VMEM((4, cases, own_rows, tb), f32),
+            pltpu.VMEM((3, cases, own_rows, tb), f32),
             pltpu.VMEM((split, cases, tb), f32),
             pltpu.VMEM((parts, cases, tb), f32),
             dma((4,)),
-            dma((4,)),
+            dma((3,)),
             dma((SENT, split - 1)),
             dma((SENT, split - 1)),
             dma((SENT, 2, split)),
@@ -396,17 +386,19 @@
             dma((parts - 1,)),
         ]
     )
-    out = jax.ShapeDtypeStruct((cases, own_rows, tb), f32)
-    return pl.pallas_call(
+    out = jax.ShapeDtypeStruct((4, cases, own_rows, tb), f32)
+    made = pl.pallas_call(
         functools.partial(kernel, parts, split),
-        out_shape=(out, out, out),
-        in_specs=[smem] * 4 + [hbm] * 5,
-        out_specs=(vmem, vmem, vmem),
+        out_shape=out,
+        in_specs=[smem] * 3 + [hbm] * 4,
+        out_specs=vmem,
         scratch_shapes=scratch,
         compiler_params=pltpu.CompilerParams(
-            collective_id=0, has_side_effects=True, vmem_limit_bytes=40 * 1024 * 1024
+            collective_id=0, has_side_effects=True, vmem_limit_bytes=63 * 1024 * 1024
         ),
-    )(rows, cols, sends, flags, tiles, right, iterate, residual, direction)
+    )(rows, cols, sends, tiles, iterate, residual, direction)
+    replaced = jnp.where(flags[:, None, None] > 0, right - made[1], made[2])
+    return iterate + made[0], replaced, made[3]
 
 
 def solution(mesh):

time: 42.4 us -> 34 us (0.80)
  local copies, waits for them, and re-layouts: 9.51 us -> 1.34 us
  Pallas kernels: 31.7 us -> 30.1 us
  other arithmetic: 0 us -> 1.44 us
    unnamed x21 -> x6, local copies, waits for them, and re-layouts: 9.51 us -> 0.01 us
    pallas_call x1, Pallas kernels: 31.7 us -> 30.1 us  [body(): pl.pallas_call(functools.partial(kernel, parts, split), out_shape=out, in...]
    select_n x0 -> x1, other arithmetic: none -> 1.43 us  [body(): replaced = jnp.where(flags[:, None, None] > 0, right - made[1], made[2])]
    squeeze x0 -> x1, local copies, waits for them, and re-layouts: none -> 1.32 us  [body(): return (iterate + made[0], replaced, made[3])]
where the time goes in v2:
time: 34 us; the launch traced here: 33.6 us
  Pallas kernels  30.1 us (89%)
  other arithmetic  1.44 us (4%)
  local copies, waits for them, and re-layouts  1.34 us (4%)
  between operations  0.7 us (2%)
    pallas_call x1, Pallas kernels, body(): pl.pallas_call(functools.partial(kernel, parts, split), out_shape=out, in...  30.1 us
    select_n x1, other arithmetic, body(): replaced = jnp.where(flags[:, None, None] > 0, right - made[1], made[2])  1.43 us
    squeeze x1, local copies, waits for them, and re-layouts, body(): return (iterate + made[0], replaced, made[3])  1.32 us

profile of v2, /device:TPU:0, one launch (start us, length us, event | category | flops | bytes accessed | tf_op | source)
XLA Modules:
  0.0 33.6 jit_solution(12731741304650306346)
XLA Ops:
  0.6 0.0 copy-start
  0.6 0.0 copy-start.2
  0.7 0.0 copy-start.1
  0.7 30.1 %shard_map.112 = f32[4,4,8,128]{3,2,1,0:T(8,128)} custom-call(s32[64]{0:T(128)} %rows_s.1, s32[64]{0:T(128)} %cols_s.1, s32[1,2,4]{2,1,0:T(2,128)} %sends_s.1, f32[64,128,128]{2,1,0:T(8,128)} %tiles_h.1, f32[4,8,128]{2,1,0:T(8,128)} %iterate_h.1, f32[4,8,128]{2,1,0:T(8,128)} %residual_h.1, f32[4,8,128]{2,1,0:T(8,128)} %direction_h.1), custom_call_target="tpu_custom_call" | custom-call | tf_op jit(solution)/shard_map/pallas_call | solution.py:390
  30.8 0.0 copy-done.2
  30.8 0.0 copy-done
  30.8 0.0 copy-done.1
  30.8 1.4 %bitcast_select_fusion = (f32[4,8,128]{2,1,0:T(8,128)}, f32[4,8,128]{2,1,0:T(8,128)}) fusion(f32[4,8,128]{2,1,0:T(8,128)S(1)} %copy-done.1, f32[4,4,8,128]{3,2,1,0:T(8,128)} %shard_map.112, pred[4]{0:T(512)(128)(4,1)S(1)} %broadcast_compare_fusion, f32[4,8,128]{2,1,0:T(8,128)S(1)} %copy-done), kind=kLoop, calls=%fused_computation | loop fusion | flops 12288 | bytes 114692 | tf_op jit(solution)/shard_map/jit(_where)/select_n | solution.py:400
  32.2 1.3 %slice_bitcast_fusion = f32[4,8,128]{2,1,0:T(8,128)} fusion(f32[4,4,8,128]{3,2,1,0:T(8,128)} %shard_map.112), kind=kLoop, calls=%fused_computation.3 | loop fusion | bytes 32768 | tf_op jit(solution)/shard_map/squeeze | solution.py:401
  (1 shorter events, 0.0 us)
Async XLA Ops:
  0.6 30.2 %copy-start = (f32[4,8,128]{2,1,0:T(8,128)S(1)}, f32[4,8,128]{2,1,0:T(8,128)}, u32[]{:S(2)}) copy-start(f32[4,8,128]{2,1,0:T(8,128)} %iterate_h.1) | copy-start | bytes 49156
  0.6 30.1 %copy-start.2 = (s32[4]{0:T(128)S(1)}, s32[4]{0:T(128)}, u32[]{:S(2)}) copy-start(s32[4]{0:T(128)} %param.13) | copy-start | bytes 52
  0.7 30.1 %copy-start.1 = (f32[4,8,128]{2,1,0:T(8,128)S(1)}, f32[4,8,128]{2,1,0:T(8,128)}, u32[]{:S(2)}) copy-start(f32[4,8,128]{2,1,0:T(8,128)} %param.14) | copy-start | bytes 49156

commit v3 on v2

--- a/solution.py
+++ b/solution.py
@@ -92,6 +92,16 @@
     base = r * own_rows
     has_left, has_right = d > 0, d < parts - 1
 
+    barrier = pltpu.get_barrier_semaphore()
+
+    def greet(dd, rr):
+        pl.semaphore_signal(barrier, inc=1, device_id=(dd, rr), device_id_type=MESH)
+
+    @pl.loop(1, parts * split)
+    def _(o):
+        to = lax.rem(d * split + r + o, parts * split)
+        greet(to // split, lax.rem(to, split))
+
     vec_copies = []
     for i, ref in enumerate((direction_h, residual_h, iterate_h)):
         copy = pltpu.make_async_copy(ref, vec_in.at[i], vec_sem.at[i])
@@ -103,28 +113,6 @@
         copy = pltpu.make_async_copy(tiles_h.at[part], tiles.at[part], tile_sem.at[i])
         copy.start()
         tile_copies.append(copy)
-
-    barrier = pltpu.get_barrier_semaphore()
-
-    def greet(dd, rr):
-        pl.semaphore_signal(barrier, inc=1, device_id=(dd, rr), device_id_type=MESH)
-
-    for o in range(1, split):
-        greet(d, lax.rem(r + o, split))
-
-    @pl.when(has_left)
-    def _():
-        for o in range(1, split):
-            greet(d - 1, lax.rem(r + o, split))
-
-    @pl.when(has_right)
-    def _():
-        for o in range(1, split):
-            greet(d + 1, lax.rem(r + o, split))
-
-    @pl.loop(1, parts)
-    def _(o):
-        greet(lax.rem(d + o, parts), r)
 
     sides = has_left.astype(jnp.int32) + has_right.astype(jnp.int32)
 
@@ -236,9 +224,9 @@
     for v in range(3):
         vec_copies[v].wait()
         stage(v, input_blocks(v))
-    pl.semaphore_wait(barrier, split - 1 + parts - 1 + (split - 1) * sides)
-    for v in range(3):
-        send(v)
+    pl.semaphore_wait(barrier, parts * split - 1)
+    send(P0)
+    send(R0)
 
     for i in range(chunks):
         tile_copies[i].wait()
@@ -276,9 +264,7 @@
     receive(R0)
     stage(R1, apply_to(R0))
     send(R1)
-    receive(X0)
-    for b, value in enumerate(apply_to(X0)):
-        image[b] = value
+    send(X0)
     payload = jnp.zeros((cases, tb), jnp.float32)
     payload = gram_of(payload, pairs_new([], [0, 1, 4, 5]))
     receive(P1)
@@ -287,48 +273,37 @@
     receive(R1)
     for b, value in enumerate(apply_to(R1)):
         own[SENT + 1][b] = value
+    receive(X0)
+    for b, value in enumerate(apply_to(X0)):
+        image[b] = value
     payload = gram_of(payload, pairs_new([0, 1, 4, 5], [2, 6]))
     receive(P2)
     for b, value in enumerate(apply_to(P2)):
         own[SENT][b] = value
     payload = gram_of(payload, pairs_new([0, 1, 2, 4, 5, 6], [3]))
 
-    gram_r[r] = payload
-
-    def gram_r_copy(o):
+    me = d * split + r
+    gram_d[me] = payload
+
+    def gram_d_copy(o):
+        to = lax.rem(me + o, parts * split)
         return pltpu.make_async_remote_copy(
-            src_ref=gram_r.at[r],
-            dst_ref=gram_r.at[r],
-            send_sem=gr_send.at[o - 1],
-            recv_sem=gr_recv.at[o - 1],
-            device_id=(d, lax.rem(r + o, split)),
+            src_ref=gram_d.at[me],
+            dst_ref=gram_d.at[me],
+            send_sem=gd_send.at[o - 1],
+            recv_sem=gd_recv.at[o - 1],
+            device_id=(to // split, lax.rem(to, split)),
             device_id_type=MESH,
         )
 
-    for o in range(1, split):
-        gram_r_copy(o).start()
-    for o in range(1, split):
-        gram_r_copy(o).wait()
-    gram_d[d] = jnp.sum(gram_r[...], axis=0)
-
-    def gram_d_copy(o):
-        return pltpu.make_async_remote_copy(
-            src_ref=gram_d.at[d],
-            dst_ref=gram_d.at[d],
-            send_sem=gd_send.at[o - 1],
-            recv_sem=gd_recv.at[o - 1],
-            device_id=(lax.rem(d + o, parts), r),
-            device_id_type=MESH,
-        )
-
-    @pl.loop(1, parts)
+    @pl.loop(1, parts * split)
     def _(o):
         gram_d_copy(o).start()
 
     for v in range(SENT):
         sent(v)
 
-    @pl.loop(1, parts)
+    @pl.loop(1, parts * split)
     def _(o):
         gram_d_copy(o).wait()
 
@@ -373,7 +348,7 @@
             pltpu.VMEM((count // 2, 2 * tb, 2 * tb), jnp.bfloat16),
             pltpu.VMEM((3, cases, own_rows, tb), f32),
             pltpu.VMEM((split, cases, tb), f32),
-            pltpu.VMEM((parts, cases, tb), f32),
+            pltpu.VMEM((parts * split, cases, tb), f32),
             dma((4,)),
             dma((3,)),
             dma((SENT, split - 1)),
@@ -382,8 +357,8 @@
             dma((SENT, 2, split)),
             dma((split - 1,)),
             dma((split - 1,)),
-            dma((parts - 1,)),
-            dma((parts - 1,)),
+            dma((parts * split - 1,)),
+            dma((parts * split - 1,)),
         ]
     )
     out = jax.ShapeDtypeStruct((4, cases, own_rows, tb), f32)

time: 34 us -> 33.6 us (0.988)
  Pallas kernels: 30.1 us -> 29.7 us
    pallas_call x1, Pallas kernels: 30.1 us -> 29.7 us  [body(): pl.pallas_call(functools.partial(kernel, parts, split), out_shape=out, in...]
where the time goes in v3:
time: 33.6 us; the launch traced here: 33.2 us
  Pallas kernels  29.7 us (88%)
  other arithmetic  1.44 us (4%)
  local copies, waits for them, and re-layouts  1.34 us (4%)
  between operations  0.7 us (2%)
    pallas_call x1, Pallas kernels, body(): pl.pallas_call(functools.partial(kernel, parts, split), out_shape=out, in...  29.7 us
    select_n x1, other arithmetic, body(): replaced = jnp.where(flags[:, None, None] > 0, right - made[1], made[2])  1.43 us
    squeeze x1, local copies, waits for them, and re-layouts, body(): return (iterate + made[0], replaced, made[3])  1.32 us

profile of v3, /device:TPU:0, one launch (start us, length us, event | category | flops | bytes accessed | tf_op | source)
XLA Modules:
  0.0 33.2 jit_solution(12248953126627319935)
XLA Ops:
  0.6 0.0 copy-start
  0.6 0.0 copy-start.2
  0.7 0.0 copy-start.1
  0.7 29.7 %shard_map.112 = f32[4,4,8,128]{3,2,1,0:T(8,128)} custom-call(s32[64]{0:T(128)} %rows_s.1, s32[64]{0:T(128)} %cols_s.1, s32[1,2,4]{2,1,0:T(2,128)} %sends_s.1, f32[64,128,128]{2,1,0:T(8,128)} %tiles_h.1, f32[4,8,128]{2,1,0:T(8,128)} %iterate_h.1, f32[4,8,128]{2,1,0:T(8,128)} %residual_h.1, f32[4,8,128]{2,1,0:T(8,128)} %direction_h.1), custom_call_target="tpu_custom_call" | custom-call | tf_op jit(solution)/shard_map/pallas_call | solution.py:365
  30.4 0.0 copy-done.2
  30.4 0.0 copy-done
  30.4 0.0 copy-done.1
  30.4 1.4 %bitcast_select_fusion = (f32[4,8,128]{2,1,0:T(8,128)}, f32[4,8,128]{2,1,0:T(8,128)}) fusion(f32[4,8,128]{2,1,0:T(8,128)S(1)} %copy-done.1, f32[4,4,8,128]{3,2,1,0:T(8,128)} %shard_map.112, pred[4]{0:T(512)(128)(4,1)S(1)} %broadcast_compare_fusion, f32[4,8,128]{2,1,0:T(8,128)S(1)} %copy-done), kind=kLoop, calls=%fused_computation | loop fusion | flops 12288 | bytes 114692 | tf_op jit(solution)/shard_map/jit(_where)/select_n | solution.py:375
  31.8 1.3 %slice_bitcast_fusion = f32[4,8,128]{2,1,0:T(8,128)} fusion(f32[4,4,8,128]{3,2,1,0:T(8,128)} %shard_map.112), kind=kLoop, calls=%fused_computation.3 | loop fusion | bytes 32768 | tf_op jit(solution)/shard_map/squeeze | solution.py:376
  (1 shorter events, 0.0 us)
Async XLA Ops:
  0.6 29.7 %copy-start = (f32[4,8,128]{2,1,0:T(8,128)S(1)}, f32[4,8,128]{2,1,0:T(8,128)}, u32[]{:S(2)}) copy-start(f32[4,8,128]{2,1,0:T(8,128)} %iterate_h.1) | copy-start | bytes 49156
  0.6 29.7 %copy-start.2 = (s32[4]{0:T(128)S(1)}, s32[4]{0:T(128)}, u32[]{:S(2)}) copy-start(s32[4]{0:T(128)} %param.13) | copy-start | bytes 52
  0.7 29.7 %copy-start.1 = (f32[4,8,128]{2,1,0:T(8,128)S(1)}, f32[4,8,128]{2,1,0:T(8,128)}, u32[]{:S(2)}) copy-start(f32[4,8,128]{2,1,0:T(8,128)} %param.14) | copy-start | bytes 49156
